TPU v7x, 32 devices: a whole 2x2x4 slice. The times are simulated.
32 devices in a mesh: energy: 8 (over z, x), tile: 4 (over y, core).
Axes of the slice: x: 2, y: 2, z: 4, core: 2. Of those that a mesh axis runs over, the one named last changes fastest.
Arguments:
- object_tiles: float32 [8, 2, 4, 512, 512], P('energy', None, 'tile'), may hold values from -6 to 6
- probe_wave: float32 [8, 2, 256, 256], P('energy'), may hold values from -6 to 6
- measured: bfloat16 [8, 4, 16, 256, 256], P('energy', 'tile'), may hold values from 0 to 2
- positions: int32 [4, 16, 2], P('tile'), may hold values from 0 to 511, as said below
- materials: float32 [2, 8, 8], replicated, may hold values from -6 to 6
Outputs:
- fitted: float32 [8, 2, 4, 512, 512], P('energy', None, 'tile')
Inputs may be any that keep to these rules, and one draw needn't show every extreme that they name: `positions`: each entry is the corner of a 256 x 256 patch, given inside its tile; in every tile some patch has row corner 512 - 1 and some has column corner 512 - 1.
All inputs are finite; a program needn't handle non-finite values.
Results may differ from a plain program's by a relative error of at most 0.0013.
Values sent between devices are 32-bit elements; how exact they have to be, the bound alone decides.
A program may use at most 64 MiB of HBM per device.

v0:
```python
import math
import jax
import jax.numpy as jnp
from jax import lax
from jax.sharding import PartitionSpec as P

TILE_COLS = 4
FIT_STEPS = 10
amplitude_floor = 0.5


def shifted(value, axis, steps):
    count = lax.axis_size(axis)
    pairs = [(source, (source + steps) % count) for source in range(count)]
    return lax.ppermute(value, axis, pairs)


def fourier_tables(length, direction):
    counter = jnp.arange(length, dtype=jnp.int32)
    products = counter[:, None] * counter[None, :] % length
    angles = 2.0 * math.pi / length * products.astype(jnp.float32)
    cosine = jnp.cos(angles)
    sine = direction * jnp.sin(angles)
    left_table = jnp.concatenate(
        [jnp.concatenate([cosine, sine], 1), jnp.concatenate([-sine, cosine], 1)], 0
    ).astype(jnp.bfloat16)
    right_table = jnp.concatenate(
        [jnp.concatenate([cosine, -sine], 1), jnp.concatenate([sine, cosine], 1)], 0
    ).astype(jnp.bfloat16)
    return (left_table, right_table)


def transform(real_part, imag_part, left_table, right_table):
    length = real_part.shape[0]
    stacked = jnp.concatenate([real_part, imag_part], 0).astype(jnp.bfloat16)
    inner = jnp.dot(left_table, stacked, preferred_element_type=jnp.float32)
    beside = jnp.concatenate([inner[:length], inner[length:]], 1).astype(jnp.bfloat16)
    outer = jnp.dot(beside, right_table, preferred_element_type=jnp.float32) / length
    return (outer[:, :length], outer[:, length:])


def patch_gradient(
    field_real, field_imag, probe_real, probe_imag, amplitude, row_start, col_start, tables
):
    length = probe_real.shape[0]
    piece_real = lax.dynamic_slice(field_real, (row_start, col_start), (length, length))
    piece_imag = lax.dynamic_slice(field_imag, (row_start, col_start), (length, length))
    exit_real = probe_real * piece_real - probe_imag * piece_imag
    exit_imag = probe_real * piece_imag + probe_imag * piece_real
    far_real, far_imag = transform(exit_real, exit_imag, tables[0], tables[1])
    magnitude = jnp.sqrt(far_real * far_real + far_imag * far_imag)
    factor = amplitude.astype(jnp.float32) / jnp.maximum(magnitude, amplitude_floor) - 1.0
    back_real, back_imag = transform(factor * far_real, factor * far_imag, tables[2], tables[3])
    return (
        probe_real * back_real + probe_imag * back_imag,
        probe_real * back_imag - probe_imag * back_real,
    )


def fit_materials(data, materials):
    high = lax.Precision.HIGHEST
    gram = jnp.einsum("rem,ren->mn", materials, materials, precision=high)
    rate = 1.0 / jnp.trace(gram)
    target = jnp.einsum("rem,rep->mp", materials, data, precision=high)

    def descend(number, coefficients):
        slope = jnp.dot(gram, coefficients, precision=high) - target
        return jnp.maximum(coefficients - rate * slope, 0.0)

    return lax.fori_loop(0, FIT_STEPS, descend, jnp.zeros_like(target))


def fitted_spectra(materials, coefficients):
    return jnp.einsum("rem,mp->rep", materials, coefficients, precision=lax.Precision.HIGHEST)


def body(object_tiles, probe_wave, measured, positions, materials):
    own_object = object_tiles[0, :, 0]
    tile_px = own_object.shape[-1]
    length = probe_wave.shape[-1]
    count = measured.shape[2]
    tile_count = lax.axis_size("tile")
    row_step = TILE_COLS % tile_count
    right_strip = shifted(own_object[:, :, :length], "tile", -1)
    widened = jnp.concatenate([own_object, right_strip], 2)
    if row_step:
        lower_strip = shifted(widened[:, :length, :], "tile", -row_step)
    else:
        lower_strip = widened[:, :length, :]
    extended = jnp.concatenate([widened, lower_strip], 1)
    forward = fourier_tables(length, 1.0)
    inverse = fourier_tables(length, -1.0)
    tables = (forward[0], forward[1], inverse[0], inverse[1])
    probe_real = probe_wave[0, 0]
    probe_imag = probe_wave[0, 1]
    own_measured = measured[0, 0]
    corners = positions[0]
    anchor = jnp.zeros((), jnp.int32)

    def accumulate(number, gradient):
        row_start = corners[number, 0]
        col_start = corners[number, 1]
        term_real, term_imag = patch_gradient(
            extended[0],
            extended[1],
            probe_real,
            probe_imag,
            own_measured[number],
            row_start,
            col_start,
            tables,
        )
        current = lax.dynamic_slice(gradient, (anchor, row_start, col_start), (2, length, length))
        return lax.dynamic_update_slice(
            gradient, current + jnp.stack([term_real, term_imag]), (anchor, row_start, col_start)
        )

    gradient = lax.fori_loop(0, count, accumulate, jnp.zeros_like(extended))
    if row_step:
        from_above = shifted(gradient[:, tile_px:, :], "tile", row_step)
    else:
        from_above = gradient[:, tile_px:, :]
    upper = jnp.concatenate(
        [gradient[:, :length, :] + from_above, gradient[:, length:tile_px, :]], 1
    )
    from_left = shifted(upper[:, :, tile_px:], "tile", 1)
    summed = jnp.concatenate([upper[:, :, :length] + from_left, upper[:, :, length:tile_px]], 2)
    peak = jnp.max(probe_real * probe_real + probe_imag * probe_imag)
    updated = own_object + summed / peak
    groups = lax.axis_size("energy")
    pixels = tile_px * tile_px
    group_width = pixels // groups
    outgoing = updated.reshape(2, 1, groups, group_width)
    arrived = lax.all_to_all(outgoing, "energy", split_axis=2, concat_axis=1, tiled=True)
    coefficients = fit_materials(arrived.reshape(2, groups, group_width), materials)
    spectra = fitted_spectra(materials, coefficients).reshape(2, groups, 1, group_width)
    returned = lax.all_to_all(spectra, "energy", split_axis=1, concat_axis=2, tiled=True)
    result = returned.reshape(2, tile_px, tile_px)
    return result.reshape(1, 2, 1, tile_px, tile_px)


def solution(mesh):
    in_specs = (
        P("energy", None, "tile", None, None),
        P("energy", None, None, None),
        P("energy", "tile", None, None, None),
        P("tile", None, None),
        P(),
    )
    out_specs = P("energy", None, "tile", None, None)
    return jax.shard_map(body, mesh=mesh, in_specs=in_specs, out_specs=out_specs, check_vma=False)
```

profile of v0, /device:TPU:0, one launch (start us, length us, event | category | flops | bytes accessed | tf_op | source)
XLA Modules:
  0.0 486.9 jit_solution(13260882390065137983)
XLA Ops:
  8.8 8.5 %collective-permute-done = f32[2,512,256]{2,1,0:T(8,128)} collective-permute-done((f32[2,512,256]{2,1,0:T(8,128)}, f32[2,512,256]{2,1,0:T(8,128)}, u32[]{:S(2)}, u32[]{:S(2)}) %collective-permute-start) | collective-permute-done | bytes 1048608 | tf_op jit(solution)/shard_map/ppermute | solution.py:15
  23.7 303.1 %while.26 = (s32[]{:T(128)}, f32[2,768,768]{2,1,0:T(8,128)}, s32[16,2]{0,1:T(2,128)S(1)}, bf16[16,256,256]{2,1,0:T(8,128)(2,1)}, f32[2,768,768]{2,1,0:T(8,128)},...) while((s32[]{:T(128)}, f32[2,768,768]{2,1,0:T(8,128)}, ...), condition=%wide.region_1.2_spmd, body=%wide.region_0.1_spmd.sunk | while | flops 541392896 | bytes 21627124 | solution.py:118
  36.0 6.3 %dynamic_update_slice.11 = f32[2,768,768]{2,1,0:T(8,128)} dynamic-update-slice(f32[2,768,768]{2,1,0:T(8,128)} %get-tuple-element.519, f32[2,256,256]{2,1,0:T(8,128)S(1)} %maximum_add_fusion.2, s32[]{:T(128)} %constant.115.clone.1..sunk, s32[]{:T(128)S(6)} %select_n.102, s32[]{:T(128)S(6)} %select_n.103) | dynamic-update-slice | bytes 1048580 | tf_op jit(solution)/shard_map/while/body/eval_jaxpr/dynamic_update_slice | solution.py:114
  54.6 6.0 %dynamic_update_slice.11 = f32[2,768,768]{2,1,0:T(8,128)} dynamic-update-slice(f32[2,768,768]{2,1,0:T(8,128)} %get-tuple-element.519, f32[2,256,256]{2,1,0:T(8,128)S(1)} %maximum_add_fusion.2, s32[]{:T(128)} %constant.115.clone.1..sunk, s32[]{:T(128)S(6)} %select_n.102, s32[]{:T(128)S(6)} %select_n.103) | dynamic-update-slice | bytes 1048580 | tf_op jit(solution)/shard_map/while/body/eval_jaxpr/dynamic_update_slice | solution.py:114
  72.9 6.8 %dynamic_update_slice.11 = f32[2,768,768]{2,1,0:T(8,128)} dynamic-update-slice(f32[2,768,768]{2,1,0:T(8,128)} %get-tuple-element.519, f32[2,256,256]{2,1,0:T(8,128)S(1)} %maximum_add_fusion.2, s32[]{:T(128)} %constant.115.clone.1..sunk, s32[]{:T(128)S(6)} %select_n.102, s32[]{:T(128)S(6)} %select_n.103) | dynamic-update-slice | bytes 1048580 | tf_op jit(solution)/shard_map/while/body/eval_jaxpr/dynamic_update_slice | solution.py:114
  92.0 6.8 %dynamic_update_slice.11 = f32[2,768,768]{2,1,0:T(8,128)} dynamic-update-slice(f32[2,768,768]{2,1,0:T(8,128)} %get-tuple-element.519, f32[2,256,256]{2,1,0:T(8,128)S(1)} %maximum_add_fusion.2, s32[]{:T(128)} %constant.115.clone.1..sunk, s32[]{:T(128)S(6)} %select_n.102, s32[]{:T(128)S(6)} %select_n.103) | dynamic-update-slice | bytes 1048580 | tf_op jit(solution)/shard_map/while/body/eval_jaxpr/dynamic_update_slice | solution.py:114
  111.1 6.7 %dynamic_update_slice.11 = f32[2,768,768]{2,1,0:T(8,128)} dynamic-update-slice(f32[2,768,768]{2,1,0:T(8,128)} %get-tuple-element.519, f32[2,256,256]{2,1,0:T(8,128)S(1)} %maximum_add_fusion.2, s32[]{:T(128)} %constant.115.clone.1..sunk, s32[]{:T(128)S(6)} %select_n.102, s32[]{:T(128)S(6)} %select_n.103) | dynamic-update-slice | bytes 1048580 | tf_op jit(solution)/shard_map/while/body/eval_jaxpr/dynamic_update_slice | solution.py:114
  130.2 6.7 %dynamic_update_slice.11 = f32[2,768,768]{2,1,0:T(8,128)} dynamic-update-slice(f32[2,768,768]{2,1,0:T(8,128)} %get-tuple-element.519, f32[2,256,256]{2,1,0:T(8,128)S(1)} %maximum_add_fusion.2, s32[]{:T(128)} %constant.115.clone.1..sunk, s32[]{:T(128)S(6)} %select_n.102, s32[]{:T(128)S(6)} %select_n.103) | dynamic-update-slice | bytes 1048580 | tf_op jit(solution)/shard_map/while/body/eval_jaxpr/dynamic_update_slice | solution.py:114
  149.2 6.6 %dynamic_update_slice.11 = f32[2,768,768]{2,1,0:T(8,128)} dynamic-update-slice(f32[2,768,768]{2,1,0:T(8,128)} %get-tuple-element.519, f32[2,256,256]{2,1,0:T(8,128)S(1)} %maximum_add_fusion.2, s32[]{:T(128)} %constant.115.clone.1..sunk, s32[]{:T(128)S(6)} %select_n.102, s32[]{:T(128)S(6)} %select_n.103) | dynamic-update-slice | bytes 1048580 | tf_op jit(solution)/shard_map/while/body/eval_jaxpr/dynamic_update_slice | solution.py:114
  168.1 6.8 %dynamic_update_slice.11 = f32[2,768,768]{2,1,0:T(8,128)} dynamic-update-slice(f32[2,768,768]{2,1,0:T(8,128)} %get-tuple-element.519, f32[2,256,256]{2,1,0:T(8,128)S(1)} %maximum_add_fusion.2, s32[]{:T(128)} %constant.115.clone.1..sunk, s32[]{:T(128)S(6)} %select_n.102, s32[]{:T(128)S(6)} %select_n.103) | dynamic-update-slice | bytes 1048580 | tf_op jit(solution)/shard_map/while/body/eval_jaxpr/dynamic_update_slice | solution.py:114
  187.1 6.9 %dynamic_update_slice.11 = f32[2,768,768]{2,1,0:T(8,128)} dynamic-update-slice(f32[2,768,768]{2,1,0:T(8,128)} %get-tuple-element.519, f32[2,256,256]{2,1,0:T(8,128)S(1)} %maximum_add_fusion.2, s32[]{:T(128)} %constant.115.clone.1..sunk, s32[]{:T(128)S(6)} %select_n.102, s32[]{:T(128)S(6)} %select_n.103) | dynamic-update-slice | bytes 1048580 | tf_op jit(solution)/shard_map/while/body/eval_jaxpr/dynamic_update_slice | solution.py:114
  206.3 6.8 %dynamic_update_slice.11 = f32[2,768,768]{2,1,0:T(8,128)} dynamic-update-slice(f32[2,768,768]{2,1,0:T(8,128)} %get-tuple-element.519, f32[2,256,256]{2,1,0:T(8,128)S(1)} %maximum_add_fusion.2, s32[]{:T(128)} %constant.115.clone.1..sunk, s32[]{:T(128)S(6)} %select_n.102, s32[]{:T(128)S(6)} %select_n.103) | dynamic-update-slice | bytes 1048580 | tf_op jit(solution)/shard_map/while/body/eval_jaxpr/dynamic_update_slice | solution.py:114
  225.4 6.6 %dynamic_update_slice.11 = f32[2,768,768]{2,1,0:T(8,128)} dynamic-update-slice(f32[2,768,768]{2,1,0:T(8,128)} %get-tuple-element.519, f32[2,256,256]{2,1,0:T(8,128)S(1)} %maximum_add_fusion.2, s32[]{:T(128)} %constant.115.clone.1..sunk, s32[]{:T(128)S(6)} %select_n.102, s32[]{:T(128)S(6)} %select_n.103) | dynamic-update-slice | bytes 1048580 | tf_op jit(solution)/shard_map/while/body/eval_jaxpr/dynamic_update_slice | solution.py:114
  244.3 6.9 %dynamic_update_slice.11 = f32[2,768,768]{2,1,0:T(8,128)} dynamic-update-slice(f32[2,768,768]{2,1,0:T(8,128)} %get-tuple-element.519, f32[2,256,256]{2,1,0:T(8,128)S(1)} %maximum_add_fusion.2, s32[]{:T(128)} %constant.115.clone.1..sunk, s32[]{:T(128)S(6)} %select_n.102, s32[]{:T(128)S(6)} %select_n.103) | dynamic-update-slice | bytes 1048580 | tf_op jit(solution)/shard_map/while/body/eval_jaxpr/dynamic_update_slice | solution.py:114
  263.4 6.8 %dynamic_update_slice.11 = f32[2,768,768]{2,1,0:T(8,128)} dynamic-update-slice(f32[2,768,768]{2,1,0:T(8,128)} %get-tuple-element.519, f32[2,256,256]{2,1,0:T(8,128)S(1)} %maximum_add_fusion.2, s32[]{:T(128)} %constant.115.clone.1..sunk, s32[]{:T(128)S(6)} %select_n.102, s32[]{:T(128)S(6)} %select_n.103) | dynamic-update-slice | bytes 1048580 | tf_op jit(solution)/shard_map/while/body/eval_jaxpr/dynamic_update_slice | solution.py:114
  282.6 6.5 %dynamic_update_slice.11 = f32[2,768,768]{2,1,0:T(8,128)} dynamic-update-slice(f32[2,768,768]{2,1,0:T(8,128)} %get-tuple-element.519, f32[2,256,256]{2,1,0:T(8,128)S(1)} %maximum_add_fusion.2, s32[]{:T(128)} %constant.115.clone.1..sunk, s32[]{:T(128)S(6)} %select_n.102, s32[]{:T(128)S(6)} %select_n.103) | dynamic-update-slice | bytes 1048580 | tf_op jit(solution)/shard_map/while/body/eval_jaxpr/dynamic_update_slice | solution.py:114
  301.4 6.6 %dynamic_update_slice.11 = f32[2,768,768]{2,1,0:T(8,128)} dynamic-update-slice(f32[2,768,768]{2,1,0:T(8,128)} %get-tuple-element.519, f32[2,256,256]{2,1,0:T(8,128)S(1)} %maximum_add_fusion.2, s32[]{:T(128)} %constant.115.clone.1..sunk, s32[]{:T(128)S(6)} %select_n.102, s32[]{:T(128)S(6)} %select_n.103) | dynamic-update-slice | bytes 1048580 | tf_op jit(solution)/shard_map/while/body/eval_jaxpr/dynamic_update_slice | solution.py:114
  320.2 6.5 %dynamic_update_slice.11 = f32[2,768,768]{2,1,0:T(8,128)} dynamic-update-slice(f32[2,768,768]{2,1,0:T(8,128)} %get-tuple-element.519, f32[2,256,256]{2,1,0:T(8,128)S(1)} %maximum_add_fusion.2, s32[]{:T(128)} %constant.115.clone.1..sunk, s32[]{:T(128)S(6)} %select_n.102, s32[]{:T(128)S(6)} %select_n.103) | dynamic-update-slice | bytes 1048580 | tf_op jit(solution)/shard_map/while/body/eval_jaxpr/dynamic_update_slice | solution.py:114
  334.5 11.9 %collective-permute-done.1 = f32[2,512,256]{2,1,0:T(8,128)} collective-permute-done((f32[2,512,256]{2,1,0:T(8,128)}, f32[2,512,256]{2,1,0:T(8,128)}, u32[]{:S(2)}, u32[]{:S(2)}) %collective-permute-start.1) | collective-permute-done | bytes 1048608 | tf_op jit(solution)/shard_map/ppermute | solution.py:15
  358.2 5.8 %all-to-all-start = ((f32[2,1,8,32768]{3,0,1,2:T(2,128)}), f32[2,1,8,32768]{3,0,1,2:T(2,128)}, u32[]{:S(2)}, u32[]{:S(2)}) async-start(f32[2,1,8,32768]{3,0,1,2:T(2,128)} %copy.11), calls=%async_computation | async-start | bytes 4194304 | tf_op jit(solution)/shard_map/all_to_all | solution.py:134
  365.6 44.6 %all-to-all-done = f32[2,1,8,32768]{3,0,1,2:T(2,128)} async-done(((f32[2,1,8,32768]{3,0,1,2:T(2,128)}), f32[2,1,8,32768]{3,0,1,2:T(2,128)}, u32[]{:S(2)}, u32[]{:S(2)}) %all-to-all-start) | async-done | bytes 2097184 | tf_op jit(solution)/shard_map/all_to_all | solution.py:134
  410.2 3.9 convolution_bitcast_fusion.1
  414.1 12.5 %while.27 = (s32[]{:T(128)}, f32[8,32768]{1,0:T(8,128)S(1)}, f32[]{:T(128)}, f32[8,8]{1,0:T(8,128)S(1)}, f32[8,32768]{1,0:T(8,128)S(1)}, /*index=5*/s32[]{:T(128)}, s32[]{:T(128)}) while((s32[]{:T(128)}, f32[8,32768]{1,0:T(8,128)S(1)}, f32[]{:T(128)}, f32[8,8]{1,0:T(8,128)S(1)}, f32[8,32768]{1,0:T(8,128)S(1)}, ...), condition=%wide.region_5.6_spmd.clone, body=%wide.region_4.5_spmd.clone.sunk | while | flops 26738692 | bytes 5243227 | solution.py:70
  430.0 51.6 %all_to_all.8 = f32[2,8,1,32768]{3,0,2,1:T(2,128)S(1)} all-to-all(f32[2,8,1,32768]{3,0,2,1:T(2,128)S(1)} %copy.14), channel_id=1, replica_groups=mesh['energy'=8,'tile'=4] {'energy'}, dimensions={1} | all-to-all | bytes 4194304 | tf_op jit(solution)/shard_map/all_to_all | solution.py:137
  (249 shorter events, 191.4 us)
Async XLA Ops:
  0.0 364.1 %copy-start = (f32[2,8,8]{2,1,0:T(8,128)S(1)}, f32[2,8,8]{2,1,0:T(8,128)}, u32[]{:S(2)}) copy-start(f32[2,8,8]{2,1,0:T(8,128)} %param.13) | copy-start | bytes 1540
  2.3 6.5 %copy-start.4 = (f32[1,2,256,256]{3,2,1,0:T(8,128)S(1)}, f32[1,2,256,256]{3,2,1,0:T(8,128)}, u32[]{:S(2)}) copy-start(f32[1,2,256,256]{3,2,1,0:T(8,128)} %param.10) | copy-start | bytes 1572868
  2.3 15.1 %collective-permute-start = (f32[2,512,256]{2,1,0:T(8,128)}, f32[2,512,256]{2,1,0:T(8,128)}, u32[]{:S(2)}, u32[]{:S(2)}) collective-permute-start(f32[2,512,256]{2,1,0:T(8,128)} %slice.152), channel_id=1, source_target_pairs={{0,3},{1,0},{2,1},{3,2},{4,7},{5,4},{6,5},{7,6},{8,11},{9,8},{10,9... | collective-permute-start | bytes 3145736 | tf_op jit(solution)/shard_map/ppermute | solution.py:15
  6.7 10.6 %copy-start.3 = (f32[1,2,1,512,512]{4,3,2,1,0:T(8,128)S(1)}, f32[1,2,1,512,512]{4,3,2,1,0:T(8,128)}, u32[]{:S(2)}) copy-start(f32[1,2,1,512,512]{4,3,2,1,0:T(8,128)} %param.9) | copy-start | bytes 6291460
  21.2 2.5 copy-start.5
  329.4 1.5 copy-start.1
  330.9 15.4 %collective-permute-start.1 = (f32[2,512,256]{2,1,0:T(8,128)}, f32[2,512,256]{2,1,0:T(8,128)}, u32[]{:S(2)}, u32[]{:S(2)}) collective-permute-start(f32[2,512,256]{2,1,0:T(8,128)} %fusion.35), channel_id=1, source_target_pairs={{0,1},{1,2},{2,3},{3,0},{4,5},{5,6},{6,7},{7,4},{8,9},{9,10},{10,1... | collective-permute-start | bytes 3145736 | tf_op jit(solution)/shard_map/ppermute | solution.py:15
  334.5 13.5 %copy-start.2 = (f32[2,256,768]{2,1,0:T(8,128)S(1)}, f32[2,256,768]{2,1,0:T(8,128)}, u32[]{:S(2)}) copy-start(f32[2,256,768]{2,1,0:T(8,128)} %copy-done.1) | copy-start | bytes 4718596
  358.2 51.9 %all-to-all-start = ((f32[2,1,8,32768]{3,0,1,2:T(2,128)}), f32[2,1,8,32768]{3,0,1,2:T(2,128)}, u32[]{:S(2)}, u32[]{:S(2)}) async-start(f32[2,1,8,32768]{3,0,1,2:T(2,128)} %copy.11), calls=%async_computation | async-start | bytes 4194304 | tf_op jit(solution)/shard_map/all_to_all | solution.py:134
where the time goes:
time: 492 us; the launch traced here: 487 us
  local copies, waits for them, and re-layouts  181 us (37%)
  waiting for transfers between devices  65 us (13%)
  other arithmetic  62.6 us (13%)
  loops' own time  62.1 us (13%)
  matrix products  56 us (11%)
  blocking collectives  51.6 us (10%)
  starting transfers between devices  8.37 us (2%)
    dynamic_update_slice x16, local copies, waits for them, and re-layouts, accumulate(): lax.dynamic_update_slice(gradient, current + jnp.stack([term_real, term_i...  106 us
    another operation x1, loops' own time, body(): gradient = lax.fori_loop(0, count, accumulate, jnp.zeros_like(extended))  61.8 us
    all_to_all x1, blocking collectives, body(): lax.all_to_all(spectra, 'energy', split_axis=1, concat_axis=2, tiled=True)  51.6 us
    all_to_all x1, waiting for transfers between devices, body(): lax.all_to_all(outgoing, 'energy', split_axis=2, concat_axis=1, tiled=True)  44.6 us
    slice x16, local copies, waits for them, and re-layouts, accumulate(): extended[0]  42.9 us
    dot_general x32, matrix products, transform(): inner = jnp.dot(left_table, stacked, preferred_element_type=jnp.float32)  27.7 us
    another operation x35, other arithmetic  23.9 us
    add x16, other arithmetic, accumulate(): current + jnp.stack([term_real, term_imag])  22 us
  transfers between devices with their start and end apart: 3, of which 3 were waited for; matrix products, arithmetic and copies ran while one was open for 2% of the time, Pallas kernels for 0%

commit v1 on v0

--- a/solution.py
+++ b/solution.py
@@ -134,7 +134,12 @@
     arrived = lax.all_to_all(outgoing, "energy", split_axis=2, concat_axis=1, tiled=True)
     coefficients = fit_materials(arrived.reshape(2, groups, group_width), materials)
     spectra = fitted_spectra(materials, coefficients).reshape(2, groups, 1, group_width)
-    returned = lax.all_to_all(spectra, "energy", split_axis=1, concat_axis=2, tiled=True)
+    returned = jnp.concatenate(
+        lax.all_to_all(
+            jnp.stack(jnp.split(spectra, lax.axis_size("energy"), axis=1)), "energy", 0, 0
+        ),
+        axis=2,
+    )
     result = returned.reshape(2, tile_px, tile_px)
     return result.reshape(1, 2, 1, tile_px, tile_px)
 

time: 492 us -> 493 us (level)
  no operation moved by 1% of the time
where the time goes in v1:
time: 493 us; the launch traced here: 487 us
  local copies, waits for them, and re-layouts  181 us (37%)
  waiting for transfers between devices  65 us (13%)
  other arithmetic  62.6 us (13%)
  loops' own time  62.1 us (13%)
  matrix products  56 us (11%)
  blocking collectives  51.6 us (10%)
  starting transfers between devices  8.37 us (2%)
    dynamic_update_slice x16, local copies, waits for them, and re-layouts, accumulate(): lax.dynamic_update_slice(gradient, current + jnp.stack([term_real, term_i...  106 us
    another operation x1, loops' own time, body(): gradient = lax.fori_loop(0, count, accumulate, jnp.zeros_like(extended))  61.8 us
    all_to_all x1, blocking collectives, body(): lax.all_to_all(jnp.stack(jnp.split(spectra, lax.axis_size('energy'), axis...  51.6 us
    all_to_all x1, waiting for transfers between devices, body(): lax.all_to_all(outgoing, 'energy', split_axis=2, concat_axis=1, tiled=True)  44.6 us
    slice x16, local copies, waits for them, and re-layouts, accumulate(): extended[0]  42.9 us
    dot_general x32, matrix products, transform(): inner = jnp.dot(left_table, stacked, preferred_element_type=jnp.float32)  27.7 us
    another operation x35, other arithmetic  23.9 us
    add x16, other arithmetic, accumulate(): current + jnp.stack([term_real, term_imag])  22 us
  transfers between devices with their start and end apart: 3, of which 3 were waited for; matrix products, arithmetic and copies ran while one was open for 2% of the time, Pallas kernels for 0%

profile of v1, /device:TPU:0, one launch (start us, length us, event | category | flops | bytes accessed | tf_op | source)
XLA Modules:
  0.0 487.1 jit_solution(17759296520986441641)
XLA Ops:
  8.8 8.5 %collective-permute-done = f32[2,512,256]{2,1,0:T(8,128)} collective-permute-done((f32[2,512,256]{2,1,0:T(8,128)}, f32[2,512,256]{2,1,0:T(8,128)}, u32[]{:S(2)}, u32[]{:S(2)}) %collective-permute-start) | collective-permute-done | bytes 1048608 | tf_op jit(solution)/shard_map/ppermute | solution.py:15
  23.7 303.1 %while.26 = (s32[]{:T(128)}, f32[2,768,768]{2,1,0:T(8,128)}, s32[16,2]{0,1:T(2,128)S(1)}, bf16[16,256,256]{2,1,0:T(8,128)(2,1)}, f32[2,768,768]{2,1,0:T(8,128)},...) while((s32[]{:T(128)}, f32[2,768,768]{2,1,0:T(8,128)}, ...), condition=%wide.region_1.2_spmd, body=%wide.region_0.1_spmd.sunk | while | flops 541392896 | bytes 21627124 | solution.py:118
  36.0 6.3 %dynamic_update_slice.11 = f32[2,768,768]{2,1,0:T(8,128)} dynamic-update-slice(f32[2,768,768]{2,1,0:T(8,128)} %get-tuple-element.519, f32[2,256,256]{2,1,0:T(8,128)S(1)} %maximum_add_fusion.2, s32[]{:T(128)} %constant.115.clone.1..sunk, s32[]{:T(128)S(6)} %select_n.102, s32[]{:T(128)S(6)} %select_n.103) | dynamic-update-slice | bytes 1048580 | tf_op jit(solution)/shard_map/while/body/eval_jaxpr/dynamic_update_slice | solution.py:114
  54.6 6.0 %dynamic_update_slice.11 = f32[2,768,768]{2,1,0:T(8,128)} dynamic-update-slice(f32[2,768,768]{2,1,0:T(8,128)} %get-tuple-element.519, f32[2,256,256]{2,1,0:T(8,128)S(1)} %maximum_add_fusion.2, s32[]{:T(128)} %constant.115.clone.1..sunk, s32[]{:T(128)S(6)} %select_n.102, s32[]{:T(128)S(6)} %select_n.103) | dynamic-update-slice | bytes 1048580 | tf_op jit(solution)/shard_map/while/body/eval_jaxpr/dynamic_update_slice | solution.py:114
  72.9 6.8 %dynamic_update_slice.11 = f32[2,768,768]{2,1,0:T(8,128)} dynamic-update-slice(f32[2,768,768]{2,1,0:T(8,128)} %get-tuple-element.519, f32[2,256,256]{2,1,0:T(8,128)S(1)} %maximum_add_fusion.2, s32[]{:T(128)} %constant.115.clone.1..sunk, s32[]{:T(128)S(6)} %select_n.102, s32[]{:T(128)S(6)} %select_n.103) | dynamic-update-slice | bytes 1048580 | tf_op jit(solution)/shard_map/while/body/eval_jaxpr/dynamic_update_slice | solution.py:114
  92.0 6.8 %dynamic_update_slice.11 = f32[2,768,768]{2,1,0:T(8,128)} dynamic-update-slice(f32[2,768,768]{2,1,0:T(8,128)} %get-tuple-element.519, f32[2,256,256]{2,1,0:T(8,128)S(1)} %maximum_add_fusion.2, s32[]{:T(128)} %constant.115.clone.1..sunk, s32[]{:T(128)S(6)} %select_n.102, s32[]{:T(128)S(6)} %select_n.103) | dynamic-update-slice | bytes 1048580 | tf_op jit(solution)/shard_map/while/body/eval_jaxpr/dynamic_update_slice | solution.py:114
  111.1 6.7 %dynamic_update_slice.11 = f32[2,768,768]{2,1,0:T(8,128)} dynamic-update-slice(f32[2,768,768]{2,1,0:T(8,128)} %get-tuple-element.519, f32[2,256,256]{2,1,0:T(8,128)S(1)} %maximum_add_fusion.2, s32[]{:T(128)} %constant.115.clone.1..sunk, s32[]{:T(128)S(6)} %select_n.102, s32[]{:T(128)S(6)} %select_n.103) | dynamic-update-slice | bytes 1048580 | tf_op jit(solution)/shard_map/while/body/eval_jaxpr/dynamic_update_slice | solution.py:114
  130.2 6.7 %dynamic_update_slice.11 = f32[2,768,768]{2,1,0:T(8,128)} dynamic-update-slice(f32[2,768,768]{2,1,0:T(8,128)} %get-tuple-element.519, f32[2,256,256]{2,1,0:T(8,128)S(1)} %maximum_add_fusion.2, s32[]{:T(128)} %constant.115.clone.1..sunk, s32[]{:T(128)S(6)} %select_n.102, s32[]{:T(128)S(6)} %select_n.103) | dynamic-update-slice | bytes 1048580 | tf_op jit(solution)/shard_map/while/body/eval_jaxpr/dynamic_update_slice | solution.py:114
  149.2 6.6 %dynamic_update_slice.11 = f32[2,768,768]{2,1,0:T(8,128)} dynamic-update-slice(f32[2,768,768]{2,1,0:T(8,128)} %get-tuple-element.519, f32[2,256,256]{2,1,0:T(8,128)S(1)} %maximum_add_fusion.2, s32[]{:T(128)} %constant.115.clone.1..sunk, s32[]{:T(128)S(6)} %select_n.102, s32[]{:T(128)S(6)} %select_n.103) | dynamic-update-slice | bytes 1048580 | tf_op jit(solution)/shard_map/while/body/eval_jaxpr/dynamic_update_slice | solution.py:114
  168.1 6.8 %dynamic_update_slice.11 = f32[2,768,768]{2,1,0:T(8,128)} dynamic-update-slice(f32[2,768,768]{2,1,0:T(8,128)} %get-tuple-element.519, f32[2,256,256]{2,1,0:T(8,128)S(1)} %maximum_add_fusion.2, s32[]{:T(128)} %constant.115.clone.1..sunk, s32[]{:T(128)S(6)} %select_n.102, s32[]{:T(128)S(6)} %select_n.103) | dynamic-update-slice | bytes 1048580 | tf_op jit(solution)/shard_map/while/body/eval_jaxpr/dynamic_update_slice | solution.py:114
  187.1 6.9 %dynamic_update_slice.11 = f32[2,768,768]{2,1,0:T(8,128)} dynamic-update-slice(f32[2,768,768]{2,1,0:T(8,128)} %get-tuple-element.519, f32[2,256,256]{2,1,0:T(8,128)S(1)} %maximum_add_fusion.2, s32[]{:T(128)} %constant.115.clone.1..sunk, s32[]{:T(128)S(6)} %select_n.102, s32[]{:T(128)S(6)} %select_n.103) | dynamic-update-slice | bytes 1048580 | tf_op jit(solution)/shard_map/while/body/eval_jaxpr/dynamic_update_slice | solution.py:114
  206.3 6.8 %dynamic_update_slice.11 = f32[2,768,768]{2,1,0:T(8,128)} dynamic-update-slice(f32[2,768,768]{2,1,0:T(8,128)} %get-tuple-element.519, f32[2,256,256]{2,1,0:T(8,128)S(1)} %maximum_add_fusion.2, s32[]{:T(128)} %constant.115.clone.1..sunk, s32[]{:T(128)S(6)} %select_n.102, s32[]{:T(128)S(6)} %select_n.103) | dynamic-update-slice | bytes 1048580 | tf_op jit(solution)/shard_map/while/body/eval_jaxpr/dynamic_update_slice | solution.py:114
  225.4 6.6 %dynamic_update_slice.11 = f32[2,768,768]{2,1,0:T(8,128)} dynamic-update-slice(f32[2,768,768]{2,1,0:T(8,128)} %get-tuple-element.519, f32[2,256,256]{2,1,0:T(8,128)S(1)} %maximum_add_fusion.2, s32[]{:T(128)} %constant.115.clone.1..sunk, s32[]{:T(128)S(6)} %select_n.102, s32[]{:T(128)S(6)} %select_n.103) | dynamic-update-slice | bytes 1048580 | tf_op jit(solution)/shard_map/while/body/eval_jaxpr/dynamic_update_slice | solution.py:114
  244.3 6.9 %dynamic_update_slice.11 = f32[2,768,768]{2,1,0:T(8,128)} dynamic-update-slice(f32[2,768,768]{2,1,0:T(8,128)} %get-tuple-element.519, f32[2,256,256]{2,1,0:T(8,128)S(1)} %maximum_add_fusion.2, s32[]{:T(128)} %constant.115.clone.1..sunk, s32[]{:T(128)S(6)} %select_n.102, s32[]{:T(128)S(6)} %select_n.103) | dynamic-update-slice | bytes 1048580 | tf_op jit(solution)/shard_map/while/body/eval_jaxpr/dynamic_update_slice | solution.py:114
  263.4 6.8 %dynamic_update_slice.11 = f32[2,768,768]{2,1,0:T(8,128)} dynamic-update-slice(f32[2,768,768]{2,1,0:T(8,128)} %get-tuple-element.519, f32[2,256,256]{2,1,0:T(8,128)S(1)} %maximum_add_fusion.2, s32[]{:T(128)} %constant.115.clone.1..sunk, s32[]{:T(128)S(6)} %select_n.102, s32[]{:T(128)S(6)} %select_n.103) | dynamic-update-slice | bytes 1048580 | tf_op jit(solution)/shard_map/while/body/eval_jaxpr/dynamic_update_slice | solution.py:114
  282.6 6.5 %dynamic_update_slice.11 = f32[2,768,768]{2,1,0:T(8,128)} dynamic-update-slice(f32[2,768,768]{2,1,0:T(8,128)} %get-tuple-element.519, f32[2,256,256]{2,1,0:T(8,128)S(1)} %maximum_add_fusion.2, s32[]{:T(128)} %constant.115.clone.1..sunk, s32[]{:T(128)S(6)} %select_n.102, s32[]{:T(128)S(6)} %select_n.103) | dynamic-update-slice | bytes 1048580 | tf_op jit(solution)/shard_map/while/body/eval_jaxpr/dynamic_update_slice | solution.py:114
  301.4 6.6 %dynamic_update_slice.11 = f32[2,768,768]{2,1,0:T(8,128)} dynamic-update-slice(f32[2,768,768]{2,1,0:T(8,128)} %get-tuple-element.519, f32[2,256,256]{2,1,0:T(8,128)S(1)} %maximum_add_fusion.2, s32[]{:T(128)} %constant.115.clone.1..sunk, s32[]{:T(128)S(6)} %select_n.102, s32[]{:T(128)S(6)} %select_n.103) | dynamic-update-slice | bytes 1048580 | tf_op jit(solution)/shard_map/while/body/eval_jaxpr/dynamic_update_slice | solution.py:114
  320.2 6.5 %dynamic_update_slice.11 = f32[2,768,768]{2,1,0:T(8,128)} dynamic-update-slice(f32[2,768,768]{2,1,0:T(8,128)} %get-tuple-element.519, f32[2,256,256]{2,1,0:T(8,128)S(1)} %maximum_add_fusion.2, s32[]{:T(128)} %constant.115.clone.1..sunk, s32[]{:T(128)S(6)} %select_n.102, s32[]{:T(128)S(6)} %select_n.103) | dynamic-update-slice | bytes 1048580 | tf_op jit(solution)/shard_map/while/body/eval_jaxpr/dynamic_update_slice | solution.py:114
  334.5 11.9 %collective-permute-done.1 = f32[2,512,256]{2,1,0:T(8,128)} collective-permute-done((f32[2,512,256]{2,1,0:T(8,128)}, f32[2,512,256]{2,1,0:T(8,128)}, u32[]{:S(2)}, u32[]{:S(2)}) %collective-permute-start.1) | collective-permute-done | bytes 1048608 | tf_op jit(solution)/shard_map/ppermute | solution.py:15
  358.2 5.8 %all-to-all-start = ((f32[2,1,8,32768]{3,0,1,2:T(2,128)}), f32[2,1,8,32768]{3,0,1,2:T(2,128)}, u32[]{:S(2)}, u32[]{:S(2)}) async-start(f32[2,1,8,32768]{3,0,1,2:T(2,128)} %copy.37), calls=%async_computation | async-start | bytes 4194304 | tf_op jit(solution)/shard_map/all_to_all | solution.py:134
  365.6 44.6 %all-to-all-done = f32[2,1,8,32768]{3,0,1,2:T(2,128)} async-done(((f32[2,1,8,32768]{3,0,1,2:T(2,128)}), f32[2,1,8,32768]{3,0,1,2:T(2,128)}, u32[]{:S(2)}, u32[]{:S(2)}) %all-to-all-start) | async-done | bytes 2097184 | tf_op jit(solution)/shard_map/all_to_all | solution.py:134
  410.2 3.9 convolution_bitcast_fusion
  414.1 12.5 %while.27 = (s32[]{:T(128)}, f32[8,32768]{1,0:T(8,128)S(1)}, f32[]{:T(128)}, f32[8,8]{1,0:T(8,128)S(1)}, f32[8,32768]{1,0:T(8,128)S(1)}, /*index=5*/s32[]{:T(128)}, s32[]{:T(128)}) while((s32[]{:T(128)}, f32[8,32768]{1,0:T(8,128)S(1)}, f32[]{:T(128)}, f32[8,8]{1,0:T(8,128)S(1)}, f32[8,32768]{1,0:T(8,128)S(1)}, ...), condition=%wide.region_5.6_spmd.clone, body=%wide.region_4.5_spmd.clone.sunk | while | flops 26738692 | bytes 5243227 | solution.py:70
  430.3 51.6 %all_to_all.14 = f32[8,2,1,1,32768]{4,2,3,1,0:T(1,128)S(1)} all-to-all(f32[8,2,1,1,32768]{4,2,3,1,0:T(1,128)S(1)} %fusion.47), channel_id=1, replica_groups=mesh['energy'=8,'tile'=4] {'energy'}, dimensions={0} | all-to-all | bytes 4194304 | tf_op jit(solution)/shard_map/all_to_all | solution.py:138
  (256 shorter events, 191.6 us)
Async XLA Ops:
  0.0 364.1 %copy-start = (f32[2,8,8]{2,1,0:T(8,128)S(1)}, f32[2,8,8]{2,1,0:T(8,128)}, u32[]{:S(2)}) copy-start(f32[2,8,8]{2,1,0:T(8,128)} %param.13) | copy-start | bytes 1540
  2.3 6.5 %copy-start.4 = (f32[1,2,256,256]{3,2,1,0:T(8,128)S(1)}, f32[1,2,256,256]{3,2,1,0:T(8,128)}, u32[]{:S(2)}) copy-start(f32[1,2,256,256]{3,2,1,0:T(8,128)} %param.10) | copy-start | bytes 1572868
  2.3 15.1 %collective-permute-start = (f32[2,512,256]{2,1,0:T(8,128)}, f32[2,512,256]{2,1,0:T(8,128)}, u32[]{:S(2)}, u32[]{:S(2)}) collective-permute-start(f32[2,512,256]{2,1,0:T(8,128)} %slice.152), channel_id=1, source_target_pairs={{0,3},{1,0},{2,1},{3,2},{4,7},{5,4},{6,5},{7,6},{8,11},{9,8},{10,9... | collective-permute-start | bytes 3145736 | tf_op jit(solution)/shard_map/ppermute | solution.py:15
  6.7 10.6 %copy-start.3 = (f32[1,2,1,512,512]{4,3,2,1,0:T(8,128)S(1)}, f32[1,2,1,512,512]{4,3,2,1,0:T(8,128)}, u32[]{:S(2)}) copy-start(f32[1,2,1,512,512]{4,3,2,1,0:T(8,128)} %param.9) | copy-start | bytes 6291460
  21.2 2.5 copy-start.5
  329.4 1.5 copy-start.1
  330.9 15.4 %collective-permute-start.1 = (f32[2,512,256]{2,1,0:T(8,128)}, f32[2,512,256]{2,1,0:T(8,128)}, u32[]{:S(2)}, u32[]{:S(2)}) collective-permute-start(f32[2,512,256]{2,1,0:T(8,128)} %fusion.35), channel_id=1, source_target_pairs={{0,1},{1,2},{2,3},{3,0},{4,5},{5,6},{6,7},{7,4},{8,9},{9,10},{10,1... | collective-permute-start | bytes 3145736 | tf_op jit(solution)/shard_map/ppermute | solution.py:15
  334.5 13.5 %copy-start.2 = (f32[2,256,768]{2,1,0:T(8,128)S(1)}, f32[2,256,768]{2,1,0:T(8,128)}, u32[]{:S(2)}) copy-start(f32[2,256,768]{2,1,0:T(8,128)} %copy-done.1) | copy-start | bytes 4718596
  358.2 51.9 %all-to-all-start = ((f32[2,1,8,32768]{3,0,1,2:T(2,128)}), f32[2,1,8,32768]{3,0,1,2:T(2,128)}, u32[]{:S(2)}, u32[]{:S(2)}) async-start(f32[2,1,8,32768]{3,0,1,2:T(2,128)} %copy.37), calls=%async_computation | async-start | bytes 4194304 | tf_op jit(solution)/shard_map/all_to_all | solution.py:134
